TPU v7x, 32 devices: a whole 2x2x4 slice. The times are simulated.
32 devices in a mesh: groups: 2 (over x), dp: 16 (over z, y, core).
Axes of the slice: x: 2, y: 2, z: 4, core: 2. Of those that a mesh axis runs over, the one named last changes fastest.
Arguments:
- images: bfloat16 [16, 128, 128, 320], P('groups', 'dp'), parts along dimension 0, may hold values from -6 to 6
- kernel_weights: bfloat16 [16, 2, 3, 3, 320, 320], P('dp'), may hold values from -0.109375 to 0.109375
- kernel_momentum: float32 [16, 2, 3, 3, 320, 320], P('dp'), may hold values from -0.12 to 0.12
- kernel_grads: bfloat16 [16, 2, 3, 3, 320, 320], P('dp'), may hold values from -0.119628906 to 0.119628906
- owners: int32 [2], replicated, may hold values from 0 to 15
Outputs:
- blocks_out: bfloat16 [16, 128, 128, 320], P('groups', 'dp'), parts along dimension 0
There are 2 independent parts, one for each index of `groups`. A program takes and returns all parts, laid end to end along the dimension named above; an argument that names none is the same for every part. Nothing has to cross between parts.
Inputs may be any that keep to these rules, and one draw needn't show every extreme that they name: `owners`: each entry is a slot index along the first dimension of the kernel state.
All inputs are finite; a program needn't handle non-finite values.
Results may differ from a plain program's by a relative error of at most 0.0095.
Values may be sent and summed in bfloat16 or wider, within the bound.
A program may use at most 128 MiB of HBM per device.

v0:
```python
import functools

import jax
import jax.numpy as jnp
from jax import lax
from jax.experimental import pallas as pl
from jax.experimental.pallas import tpu as pltpu
from jax.sharding import PartitionSpec as P

momentum_decay = 0.9
learn_rate = 0.5
MESH = pl.DeviceIdType.MESH
fine_chunks = 15
coarse_chunks = 9
pair_hop = 2
hop = 3
slow_hop = 4


class Place:
    def __init__(self, groups, dp):
        self.groups, self.dp, self.last = groups, dp, dp // 4 - 1
        self.group, self.at = lax.axis_index("groups"), lax.axis_index("dp")
        self.z, self.y, self.core = self.at // 4, (self.at // 2) % 2, self.at % 2
        self.mate = self.at + 1 - 2 * self.core
        self.beside = self.at - 1 + 2 * self.core
        self.across = self.at + 2 - 4 * self.y
        self.share = 2 * self.group + self.core
        self.others = [lax.rem(self.group + step, groups) for step in range(1, groups)]
        self.has_beside = (self.beside >= 0) & (self.beside < dp)

    def meet(self):
        barrier = pltpu.get_barrier_semaphore()

        def greet(**where):
            pl.semaphore_signal(barrier, inc=1, device_id=where, device_id_type=MESH)

        greet(dp=self.mate)
        greet(dp=self.across)
        for other in self.others:
            greet(groups=other)
        pl.when(self.has_beside)(lambda: greet(dp=self.beside))
        pl.when(self.z > 0)(lambda: greet(dp=self.at - 4))
        pl.when(self.z < self.last)(lambda: greet(dp=self.at + 4))
        more = [
            jnp.where(there, 1, 0)
            for there in (self.has_beside, self.z > 0, self.z < self.last)
        ]
        pl.semaphore_wait(barrier, 1 + self.groups + sum(more))


def remote(src, dst, sem, k, **where):
    return pltpu.make_async_remote_copy(
        src, dst, sem.at[0, k], sem.at[1, k], device_id=where, device_id_type=MESH
    )


class Stream:
    def __init__(self, place, col, out, col_in, joined, fwd, fwd_in, back, back_in, done, sems):
        self.__dict__.update(place=place, col=col, out=out, col_in=col_in, joined=joined)
        self.__dict__.update(fwd=fwd, fwd_in=fwd_in, back=back, back_in=back_in, done=done)
        self.col_sem, self.fwd_sem, self.back_sem, self.mate_sem = sems[:4]
        self.cross_sem, self.pass_sem, self.keep_sem = sems[4:]

    def to_col(self, k):
        return remote(self.col.at[k], self.col_in.at[k], self.col_sem, k, dp=self.place.across)

    def to_fwd(self, k, up=4):
        return remote(self.fwd.at[k], self.fwd_in.at[k], self.fwd_sem, k, dp=self.place.at + up)

    def to_back(self, k, down=4):
        return remote(self.back.at[k], self.back_in.at[k], self.back_sem, k, dp=self.place.at - down)

    def keep(self, k):
        return pltpu.make_async_copy(
            self.done.at[k], self.out.at[k, self.place.share], self.keep_sem.at[k]
        )

    def to_mate(self, k):
        return remote(
            self.done.at[k], self.out.at[k, self.place.share], self.mate_sem, k, dp=self.place.mate
        )

    def to_cross(self, k, i):
        return remote(
            self.done.at[k], self.out.at[k, self.place.share], self.cross_sem.at[i], k,
            groups=self.place.others[i],
        )

    def to_pass(self, k, i):
        p = self.place
        slot = 2 * lax.rem(p.group + p.groups - 1 - i, p.groups) + p.core
        return remote(self.out.at[k, slot], self.out.at[k, slot], self.pass_sem.at[i], k, dp=p.mate)

    def join_col(self, k):
        self.to_col(k).wait_recv()
        self.joined[k] = self.col[k] + self.col_in[k]

    def go_fwd(self, k):
        p = self.place

        @pl.when(p.z == 0)
        def _():
            self.fwd[k] = self.joined[k]

        @pl.when(p.z > 0)
        def _():
            self.to_fwd(k, -4).wait_recv()
            self.fwd[k] = self.joined[k] + self.fwd_in[k]

        pl.when(p.z < p.last)(lambda: self.to_fwd(k).start())

    def go_back(self, k):
        p = self.place

        @pl.when(p.z == p.last)
        def _():
            self.back[k] = self.joined[k]

        @pl.when(p.z < p.last)
        def _():
            self.to_back(k, -4).wait_recv()
            self.back[k] = self.joined[k] + self.back_in[k]

        pl.when(p.z > 0)(lambda: self.to_back(k).start())

    def finish(self, k):
        p = self.place

        @pl.when(p.z < p.last)
        def _():
            self.done[k] = self.fwd[k] + self.back_in[k]

        @pl.when(p.z == p.last)
        def _():
            self.done[k] = self.fwd[k]

        for i in range(p.groups - 1):
            self.to_cross(k, i).start()
        self.to_mate(k).start()
        self.keep(k).start()

    def pass_on(self, k):
        for i in range(self.place.groups - 1):
            self.to_cross(k, i).wait_recv()
            self.to_pass(k, i).start()

    def steps(self, chunks, hop):
        return chunks + hop * (self.place.last + 2)

    def step(self, t, chunks, hop):
        p = self.place
        at_step(t - hop, chunks, self.join_col)
        at_step(t - hop - p.z * hop, chunks, self.go_fwd)
        at_step(t - hop - (p.last - p.z) * hop, chunks, self.go_back)
        at_step(t - hop - p.last * hop, chunks, self.finish)
        at_step(t - hop - p.last * hop - hop, chunks, self.pass_on)

    def drain(self, k):
        p = self.place
        self.to_col(k).wait_send()
        pl.when(p.z < p.last)(lambda: self.to_fwd(k).wait_send())
        pl.when(p.z > 0)(lambda: self.to_back(k).wait_send())
        self.to_mate(k).wait()
        self.keep(k).wait()
        for i in range(p.groups - 1):
            self.to_cross(k, i).wait_send()
            self.to_pass(k, i).wait()

    @staticmethod
    def scratch(chunks, part, width, groups):
        piece = pltpu.VMEM((chunks, part, width), jnp.bfloat16)
        sems = pltpu.SemaphoreType.DMA((2, chunks))
        many = pltpu.SemaphoreType.DMA((groups - 1, 2, chunks))
        return [piece] * 7 + [sems] * 4 + [many] * 2 + [pltpu.SemaphoreType.DMA((chunks,))]


def half_rows(part):
    return -(-(part // 2) // 8) * 8


def packed_rows(part, width):
    return width // 128 * part + (half_rows(part) if width % 128 else 0)


def packed(v):
    part, width = v.shape
    full, half = width // 128 * 128, half_rows(part)
    blocks = [v[:, i : i + 128] for i in range(0, full, 128)]
    if full < width:
        low, high = v[:half, full:], v[half:, full:]
        if part < 2 * half:
            high = jnp.concatenate(
                [high, jnp.zeros((2 * half - part, width - full), v.dtype)], axis=0
            )
        blocks.append(jnp.concatenate([low, high], axis=1))
    return jnp.concatenate(blocks, axis=0)


def unpack(k_ref, natural):
    chunks, shares, _, _ = k_ref.shape
    depth, width = natural.shape
    part = depth // (chunks * shares)
    full, half = width // 128 * 128, half_rows(part)
    for piece in range(chunks * shares):
        v = k_ref[piece // shares, piece % shares].astype(jnp.float32)
        base = piece * part
        for i in range(full // 128):
            natural[base : base + part, i * 128 : (i + 1) * 128] = v[i * part : (i + 1) * part]
        if full < width:
            rest = v[full // 128 * part :]
            natural[base : base + half, full:] = rest[:, : width - full]
            natural[base + half : base + part, full:] = rest[: part - half, width - full :]


def at_step(k, chunks, what):
    pl.when((k >= 0) & (k < chunks))(lambda: what(k))


def each(chunks, what):
    def body(k, carry):
        what(k)
        return carry

    lax.fori_loop(0, chunks, body, 0)


class Edges:
    def __init__(self, place, first, final, out, sem):
        self.place, self.first, self.final, self.out, self.sem = place, first, final, out, sem

    def down(self, k, to=1):
        return remote(self.final(k), self.out(0, k), self.sem.at[0], k, dp=self.place.at + to)

    def up(self, k, to=1):
        return remote(self.first(k), self.out(1, k), self.sem.at[1], k, dp=self.place.at - to)

    def start(self, k):
        at, dp = self.place.at, self.place.dp
        pl.when(at < dp - 1)(lambda: self.down(k).start())
        pl.when(at > 0)(lambda: self.up(k).start())

    def drain(self, k):
        at, dp = self.place.at, self.place.dp

        @pl.when(at < dp - 1)
        def _():
            self.down(k).wait_send()
            self.up(k, -1).wait_recv()

        @pl.when(at > 0)
        def _():
            self.up(k).wait_send()
            self.down(k, -1).wait_recv()


class Renewal:
    def __init__(self, place, mask, base, state, bufs, col, pair_out, pair_in, load_sem, pair_sem):
        self.place, self.mask, self.base = place, mask, base
        self.state, self.bufs = state, bufs
        self.col, self.pair_out, self.pair_in = col, pair_out, pair_in
        self.load_sem, self.pair_sem = load_sem, pair_sem

    def loads(self, k):
        src = pl.ds(2 * self.place.group, 2)
        return [
            pltpu.make_async_copy(ref.at[self.base + k, src], buf.at[k], self.load_sem.at[i, k])
            for i, (ref, buf) in enumerate(zip(self.state, self.bufs))
        ]

    def start(self, k):
        for copy in self.loads(k):
            copy.start()

    def to_pair(self, k):
        return remote(
            self.pair_out.at[k], self.pair_in.at[k], self.pair_sem, k, dp=self.place.mate
        )

    def renew(self, k):
        for copy in self.loads(k):
            copy.wait()
        w, m, g = self.bufs
        mine = self.mask > 0.5

        def new(c):
            velocity = momentum_decay * m[k, c] + g[k, c].astype(jnp.float32)
            updated = w[k, c].astype(jnp.float32) - learn_rate * velocity
            return packed(jnp.where(mine, updated, 0.0)).astype(jnp.bfloat16)

        self.pair_out[k] = new(1 - self.place.core)
        self.to_pair(k).start()
        self.col[k] = new(self.place.core)

    def join(self, k):
        self.to_pair(k).wait_recv()
        self.col[k] = self.col[k] + self.pair_in[k]

    @staticmethod
    def scratch(chunks, part, width):
        load = lambda dtype: pltpu.VMEM((chunks, 2, part, width), dtype)
        piece = pltpu.VMEM((chunks, packed_rows(part, width), 128), jnp.bfloat16)
        return [load(jnp.bfloat16), load(jnp.float32), load(jnp.bfloat16), piece, piece] + [
            pltpu.SemaphoreType.DMA((3, chunks)),
            pltpu.SemaphoreType.DMA((2, chunks)),
        ]


def spread_kernel(groups, dp, mask_ref, *refs):
    first_state, second_state, x_ref, out_ref, col1_ref, rims_ref = (
        refs[:3], refs[3:6], refs[6], refs[7], refs[8], refs[9],
    )
    scratch = refs[10:]
    place = Place(groups, dp)
    one = Renewal(place, mask_ref[0], 0, first_state, scratch[:3], scratch[14], *scratch[3:7])
    two = Renewal(place, mask_ref[1], coarse_chunks, second_state, scratch[7:10], col1_ref, *scratch[10:14])
    stream = Stream(place, scratch[14], out_ref, *scratch[15:22], scratch[22:29])
    height = x_ref.shape[1]
    edges = Edges(
        place, lambda k: x_ref.at[:, 0], lambda k: x_ref.at[:, height - 1],
        lambda side, k: rims_ref.at[side], scratch[29],
    )
    each(fine_chunks, one.start)
    each(coarse_chunks, two.start)
    place.meet()

    def join(k):
        one.join(k)
        stream.to_col(k).start()

    def step(t, carry):
        at_step(t, fine_chunks, one.renew)
        at_step(t - pair_hop, fine_chunks, join)
        stream.step(t - pair_hop, fine_chunks, hop)
        late = t - fine_chunks - pair_hop
        pl.when(late == 0)(lambda: edges.start(0))
        at_step(late - 1, coarse_chunks, two.renew)
        at_step(late - 1 - pair_hop, coarse_chunks, two.join)
        return carry

    ends = (pair_hop + stream.steps(fine_chunks, hop), fine_chunks + coarse_chunks + 2 * pair_hop + 1)
    lax.fori_loop(0, max(ends), step, 0)

    def drain(k):
        one.to_pair(k).wait_send()
        stream.drain(k)

    each(fine_chunks, drain)
    each(coarse_chunks, lambda k: two.to_pair(k).wait_send())
    edges.drain(0)


def spread(kernel_weights, kernel_momentum, kernel_grads, owners, x):
    groups, dp = lax.axis_size("groups"), lax.axis_size("dp")
    _, _, rows, columns, fan_in, fan_out = kernel_weights.shape
    images, _, channels, width = x.shape
    shares, depth = 2 * groups, rows * columns * fan_in
    mine = (owners == lax.axis_index("dp")).astype(jnp.float32)
    mask = jnp.broadcast_to(mine[:, None, None], (2, 1, fan_out))
    state = (kernel_weights, kernel_momentum, kernel_grads)

    def cut(chunks):
        return [a.reshape(2 * chunks, shares, -1, fan_out) for a in state]

    fine, coarse = depth // fine_chunks // shares, depth // coarse_chunks // shares
    fine_rows, coarse_rows = packed_rows(fine, fan_out), packed_rows(coarse, fan_out)
    any_space = pl.BlockSpec(memory_space=pl.ANY)
    vmem = pl.BlockSpec(memory_space=pltpu.VMEM)
    kernel, col, rims = pl.pallas_call(
        functools.partial(spread_kernel, groups, dp),
        out_shape=[
            jax.ShapeDtypeStruct((fine_chunks, shares, fine_rows, 128), jnp.bfloat16),
            jax.ShapeDtypeStruct((coarse_chunks, coarse_rows, 128), jnp.bfloat16),
            jax.ShapeDtypeStruct((2, images, channels, width), jnp.bfloat16),
        ],
        in_specs=[vmem] + [any_space] * 7,
        out_specs=[vmem, vmem, any_space],
        scratch_shapes=Renewal.scratch(fine_chunks, fine, fan_out)
        + Renewal.scratch(coarse_chunks, coarse, fan_out)
        + [pltpu.VMEM((fine_chunks, fine_rows, 128), jnp.bfloat16)]
        + Stream.scratch(fine_chunks, fine_rows, 128, groups)
        + [pltpu.SemaphoreType.DMA((2, 2, 1))],
        compiler_params=pltpu.CompilerParams(
            collective_id=0, has_side_effects=True, vmem_limit_bytes=56 << 20
        ),
    )(mask, *cut(fine_chunks), *cut(coarse_chunks), x)
    return kernel, col, rims


def silu(v):
    return v / (1.0 + jnp.exp(-v))


def conv_image(x_ref, top_ref, bottom_ref, o_ref, patch, wide, between=lambda row: None):
    height, channels, width = x_ref.shape
    at = lax.axis_index("dp")
    column = lax.broadcasted_iota(jnp.int32, (1, width), 1)

    def build(row):
        if row == 0:
            v = jnp.where(at > 0, top_ref[...].astype(jnp.float32), 0.0)
        elif row == height + 1:
            v = jnp.where(at < lax.axis_size("dp") - 1, bottom_ref[...].astype(jnp.float32), 0.0)
        else:
            v = x_ref[row - 1]
        a = silu(v.astype(jnp.float32))
        before = jnp.where(column == 0, 0.0, pltpu.roll(a, 1, 1))
        after = jnp.where(column == width - 1, 0.0, pltpu.roll(a, width - 1, 1))
        for dc, part in enumerate((before, a, after)):
            patch[row, dc * channels : (dc + 1) * channels] = part.astype(jnp.bfloat16)

    built = 0
    for row in range(0, height, 2):
        between(row)
        while built < row + 4:
            build(built)
            built += 1
        rhs = jnp.concatenate(
            [
                jnp.concatenate([patch[row + dr], patch[row + dr + 1]], axis=1)
                for dr in range(3)
            ],
            axis=0,
        )
        acc = jnp.dot(wide[...], rhs, preferred_element_type=jnp.float32)
        for i in range(2):
            x = x_ref[row + i].astype(jnp.float32)
            o_ref[row + i] = (x + acc[:, i * width : (i + 1) * width]).astype(o_ref.dtype)


def first_kernel(groups, dp, x_ref, top_ref, bottom_ref, k_ref, col_ref, o_ref, out_ref, rims_ref,
                 patch, wide, natural, borders, edge_sem, *scratch):
    place = Place(groups, dp)
    image, images = pl.program_id(0), pl.num_programs(0)
    height = x_ref.shape[1]
    stream = Stream(place, col_ref, out_ref, *scratch[:7], scratch[7:])
    edges = Edges(
        place, lambda k: borders.at[k, 0], lambda k: borders.at[k, 1],
        lambda side, k: rims_ref.at[side, k], edge_sem,
    )

    @pl.when(image == 0)
    def _():
        place.meet()
        unpack(k_ref, natural)
        wide[...] = natural[...].T.astype(jnp.bfloat16)

    def step(t, carry=0):
        at_step(t, coarse_chunks, lambda k: stream.to_col(k).start())
        stream.step(t, coarse_chunks, slow_hop)
        return carry

    def between(row):
        if row % (height // 2) == 0:
            now = 4 * image + row // (height // 2) * 2
            step(now)
            step(now + 1)

    conv_image(x_ref.at[0], top_ref.at[0, 0], bottom_ref.at[0, 0], o_ref.at[0], patch, wide, between)
    borders[image, 0] = o_ref[0, 0]
    borders[image, 1] = o_ref[0, height - 1]
    edges.start(image)

    @pl.when(image == images - 1)
    def _():
        count = borders.shape[0]
        lax.fori_loop(4 * count, max(4 * count, stream.steps(coarse_chunks, slow_hop)), step, 0)
        each(coarse_chunks, stream.drain)
        each(count, edges.drain)


def second_kernel(x_ref, top_ref, bottom_ref, k_ref, o_ref, patch, wide, natural):
    @pl.when(pl.program_id(0) == 0)
    def _():
        unpack(k_ref, natural)
        wide[...] = natural[...].T.astype(jnp.bfloat16)

    conv_image(x_ref.at[0], top_ref.at[0, 0], bottom_ref.at[0, 0], o_ref.at[0], patch, wide)


def conv_specs(x, kernel):
    images, height, channels, width = x.shape
    image = pl.BlockSpec((1, height, channels, width), lambda i: (i, 0, 0, 0))
    top = pl.BlockSpec((1, 1, channels, width), lambda i: (0, i, 0, 0))
    bottom = pl.BlockSpec((1, 1, channels, width), lambda i: (1, i, 0, 0))
    scratch = [
        pltpu.VMEM((height + 2, 3 * channels, width), jnp.bfloat16),
        pltpu.VMEM((channels, 9 * channels), jnp.bfloat16),
        pltpu.VMEM((9 * channels, channels), jnp.float32),
    ]
    whole = pl.BlockSpec(kernel.shape, lambda i: (0, 0, 0, 0))
    return image, [image, top, bottom, whole], scratch


def first_conv(x, rims, kernel, col):
    groups, dp = lax.axis_size("groups"), lax.axis_size("dp")
    images, height, channels, width = x.shape
    chunks, part, fan_out = col.shape
    image, in_specs, scratch = conv_specs(x, kernel)
    any_space = pl.BlockSpec(memory_space=pl.ANY)
    hidden, second, rims = pl.pallas_call(
        functools.partial(first_kernel, groups, dp),
        out_shape=[
            jax.ShapeDtypeStruct(x.shape, x.dtype),
            jax.ShapeDtypeStruct((chunks, 2 * groups, part, fan_out), jnp.bfloat16),
            jax.ShapeDtypeStruct(rims.shape, rims.dtype),
        ],
        grid=(images,),
        in_specs=in_specs + [pl.BlockSpec(col.shape, lambda i: (0, 0, 0))],
        out_specs=[image, any_space, any_space],
        scratch_shapes=scratch
        + [
            pltpu.VMEM((images, 2, channels, width), jnp.bfloat16),
            pltpu.SemaphoreType.DMA((2, 2, images)),
        ]
        + Stream.scratch(chunks, part, fan_out, groups),
        compiler_params=pltpu.CompilerParams(
            collective_id=1, has_side_effects=True, vmem_limit_bytes=56 << 20
        ),
    )(x, rims, rims, kernel, col)
    return hidden, second, rims


def second_conv(x, rims, kernel):
    image, in_specs, scratch = conv_specs(x, kernel)
    return pl.pallas_call(
        second_kernel,
        out_shape=jax.ShapeDtypeStruct(x.shape, x.dtype),
        grid=(x.shape[0],),
        in_specs=in_specs,
        out_specs=image,
        scratch_shapes=scratch,
        compiler_params=pltpu.CompilerParams(vmem_limit_bytes=56 << 20),
    )(x, rims, rims, kernel)


def local(images, kernel_weights, kernel_momentum, kernel_grads, owners):
    x = images.transpose(0, 1, 3, 2)
    kernel, col, rims = spread(kernel_weights, kernel_momentum, kernel_grads, owners, x)
    hidden, kernel, rims = first_conv(x, rims, kernel, col)
    return second_conv(hidden, rims, kernel).transpose(0, 1, 3, 2)


def solution(mesh):
    placed = (
        P("groups", "dp", None, None),
        P("dp", None, None, None, None, None),
        P("dp", None, None, None, None, None),
        P("dp", None, None, None, None, None),
        P(),
    )
    return jax.shard_map(
        local, mesh=mesh, in_specs=placed, out_specs=P("groups", "dp", None, None), check_vma=False
    )
```

profile of v0, /device:TPU:1, one launch (start us, length us, event | category | flops | bytes accessed | tf_op | source)
XLA Modules:
  0.0 114.1 jit_solution(16567289108769379293)
XLA Ops:
  0.0 0.7 compare_convert_fusion
  0.7 0.7 broadcast_in_dim.2.mask_ref
  1.3 45.9 %shard_map.55 = (bf16[15,4,120,128]{3,2,1,0:T(8,128)(2,1)}, bf16[9,200,128]{2,1,0:T(8,128)(2,1)}, bf16[2,8,320,128]{3,2,1,0:T(8,128)(2,1)}) custom-call(f32[2,1,320]{2,1,0:T(1,128)} %broadcast_in_dim.2.mask_ref, bf16[30,4,48,320]{3,2,1,0:T(8,128)(2,1)} %bitcast.12, f32[30,4,48,320]{3,2,1,0:T(8,128)} %bitcast.8, bf16[30,4,48,320]{3,2,1,0:T(8,128)(2,1)} %bitcast.14, ...), custom_call_target="tpu_custom_call" | custom-call | tf_op jit(solution)/shard_map/pallas_call | solution.py:369
  47.2 43.4 %shard_map.56 = (bf16[8,8,320,128]{3,2,1,0:T(8,128)(2,1)}, bf16[9,4,200,128]{3,2,1,0:T(8,128)(2,1)}, bf16[2,8,320,128]{3,2,1,0:T(8,128)(2,1)}) custom-call(bf16[8,8,320,128]{3,2,1,0:T(8,128)(2,1)} %bitcast.11, bf16[2,8,320,128]{3,2,1,0:T(8,128)(2,1)} %get-tuple-element.11.top_ref.bottom_ref, bf16[2,8,320,128]{3,2,1,0:T(8,128)(2,1)} %get-tuple-element.11.top_ref.bottom_ref, ...), custom_call_target="tpu_custom_call" | custom-call | tf_op jit(solution)/shard_map/pallas_call | solution.py:501
  90.7 23.4 %shard_map.57 = bf16[8,8,320,128]{3,2,1,0:T(8,128)(2,1)} custom-call(bf16[8,8,320,128]{3,2,1,0:T(8,128)(2,1)} %get-tuple-element.14.x_ref, bf16[2,8,320,128]{3,2,1,0:T(8,128)(2,1)} %get-tuple-element.15.top_ref.bottom_ref, bf16[2,8,320,128]{3,2,1,0:T(8,128)(2,1)} %get-tuple-element.15.top_ref.bottom_ref, bf16[9,4,200,128]{3,2,1,0:T(8,128)(2,1)} %get-tuple-element.16.k_ref), custom_call_target="tpu_custom_call" | custom-call | tf_op jit(solution)/shard_map/pallas_call | solution.py:526
where the time goes:
time: 114 us
  Pallas kernels  113 us (99%)
    pallas_call x1, Pallas kernels, spread(): pl.pallas_call(functools.partial(spread_kernel, groups, dp), out_shape=[j...  45.9 us
    pallas_call x1, Pallas kernels, first_conv(): pl.pallas_call(functools.partial(first_kernel, groups, dp), out_shape=[ja...  43.4 us
    pallas_call x1, Pallas kernels, second_conv(): pl.pallas_call(second_kernel, out_shape=jax.ShapeDtypeStruct(x.shape, x.d...  23.4 us

commit v1 on v0

--- a/solution.py
+++ b/solution.py
@@ -12,8 +12,8 @@
 MESH = pl.DeviceIdType.MESH
 fine_chunks = 15
 coarse_chunks = 9
-pair_hop = 2
-hop = 3
+pair_hop = 3
+hop = 6
 slow_hop = 4
 
 

time: 114 us -> 115 us (level)
  no operation moved by 1% of the time
where the time goes in v1:
time: 115 us
  Pallas kernels  113 us (98%)
    pallas_call x1, Pallas kernels, spread(): pl.pallas_call(functools.partial(spread_kernel, groups, dp), out_shape=[j...  45.7 us
    pallas_call x1, Pallas kernels, first_conv(): pl.pallas_call(functools.partial(first_kernel, groups, dp), out_shape=[ja...  44.4 us
    pallas_call x1, Pallas kernels, second_conv(): pl.pallas_call(second_kernel, out_shape=jax.ShapeDtypeStruct(x.shape, x.d...  23.4 us

profile of v1, /device:TPU:1, one launch (start us, length us, event | category | flops | bytes accessed | tf_op | source)
XLA Modules:
  0.0 114.8 jit_solution(11855217180578139370)
XLA Ops:
  0.0 0.7 compare_convert_fusion
  0.7 0.7 broadcast_in_dim.2.mask_ref
  1.3 45.7 %shard_map.55 = (bf16[15,4,120,128]{3,2,1,0:T(8,128)(2,1)}, bf16[9,200,128]{2,1,0:T(8,128)(2,1)}, bf16[2,8,320,128]{3,2,1,0:T(8,128)(2,1)}) custom-call(f32[2,1,320]{2,1,0:T(1,128)} %broadcast_in_dim.2.mask_ref, bf16[30,4,48,320]{3,2,1,0:T(8,128)(2,1)} %bitcast.12, f32[30,4,48,320]{3,2,1,0:T(8,128)} %bitcast.8, bf16[30,4,48,320]{3,2,1,0:T(8,128)(2,1)} %bitcast.14, ...), custom_call_target="tpu_custom_call" | custom-call | tf_op jit(solution)/shard_map/pallas_call | solution.py:369
  47.0 44.4 %shard_map.56 = (bf16[8,8,320,128]{3,2,1,0:T(8,128)(2,1)}, bf16[9,4,200,128]{3,2,1,0:T(8,128)(2,1)}, bf16[2,8,320,128]{3,2,1,0:T(8,128)(2,1)}) custom-call(bf16[8,8,320,128]{3,2,1,0:T(8,128)(2,1)} %bitcast.11, bf16[2,8,320,128]{3,2,1,0:T(8,128)(2,1)} %get-tuple-element.11.top_ref.bottom_ref, bf16[2,8,320,128]{3,2,1,0:T(8,128)(2,1)} %get-tuple-element.11.top_ref.bottom_ref, ...), custom_call_target="tpu_custom_call" | custom-call | tf_op jit(solution)/shard_map/pallas_call | solution.py:501
  91.4 23.4 %shard_map.57 = bf16[8,8,320,128]{3,2,1,0:T(8,128)(2,1)} custom-call(bf16[8,8,320,128]{3,2,1,0:T(8,128)(2,1)} %get-tuple-element.14.x_ref, bf16[2,8,320,128]{3,2,1,0:T(8,128)(2,1)} %get-tuple-element.15.top_ref.bottom_ref, bf16[2,8,320,128]{3,2,1,0:T(8,128)(2,1)} %get-tuple-element.15.top_ref.bottom_ref, bf16[9,4,200,128]{3,2,1,0:T(8,128)(2,1)} %get-tuple-element.16.k_ref), custom_call_target="tpu_custom_call" | custom-call | tf_op jit(solution)/shard_map/pallas_call | solution.py:526

commit v2 on v1

v2 whole, which is shorter than its diff:
```python
import functools

import jax
import jax.numpy as jnp
from jax import lax
from jax.experimental import pallas as pl
from jax.experimental.pallas import tpu as pltpu
from jax.sharding import PartitionSpec as P

momentum_decay = 0.9
learn_rate = 0.5
MESH = pl.DeviceIdType.MESH
fine_chunks = 15
coarse_chunks = 5
pair_hop = 3
fine_hop = 5
coarse_hop = 2
coarse_stride = 3
edge_start = 18
edge_stride = 3
build_back = 8
near, far = 0.75, 1.5
log2_e = 1.4426950408889634


class Place:
    def __init__(self, groups, dp):
        self.groups, self.dp, self.last = groups, dp, dp // 4 - 1
        self.group, self.at = lax.axis_index("groups"), lax.axis_index("dp")
        self.z, self.y, self.core = self.at // 4, (self.at // 2) % 2, self.at % 2
        self.mate = self.at + 1 - 2 * self.core
        self.beside = self.at - 1 + 2 * self.core
        self.across = self.at + 2 - 4 * self.y
        self.share = 2 * self.group + self.core
        self.others = [lax.rem(self.group + step, groups) for step in range(1, groups)]
        self.has_beside = (self.beside >= 0) & (self.beside < dp)

    def meet(self):
        barrier = pltpu.get_barrier_semaphore()

        def greet(**where):
            pl.semaphore_signal(barrier, inc=1, device_id=where, device_id_type=MESH)

        greet(dp=self.mate)
        greet(dp=self.across)
        for other in self.others:
            greet(groups=other)
        pl.when(self.has_beside)(lambda: greet(dp=self.beside))
        pl.when(self.z > 0)(lambda: greet(dp=self.at - 4))
        pl.when(self.z < self.last)(lambda: greet(dp=self.at + 4))
        more = [
            jnp.where(there, 1, 0)
            for there in (self.has_beside, self.z > 0, self.z < self.last)
        ]
        pl.semaphore_wait(barrier, 1 + self.groups + sum(more))


def remote(src, dst, sem, k, **where):
    return pltpu.make_async_remote_copy(
        src, dst, sem.at[0, k], sem.at[1, k], device_id=where, device_id_type=MESH
    )


def at_step(k, chunks, what):
    pl.when((k >= 0) & (k < chunks))(lambda: what(k))


def at_stride(k, stride, chunks, what):
    pl.when((k >= 0) & (k % stride == 0) & (k < chunks * stride))(lambda: what(k // stride))


def each(chunks, what):
    def body(k, carry):
        what(k)
        return carry

    lax.fori_loop(0, chunks, body, 0)


def half_rows(part):
    return -(-(part // 2) // 8) * 8


def packed_rows(part, width):
    return width // 128 * part + (half_rows(part) if width % 128 else 0)


def packed(v):
    part, width = v.shape
    full, half = width // 128 * 128, half_rows(part)
    blocks = [v[:, i : i + 128] for i in range(0, full, 128)]
    if full < width:
        low, high = v[:half, full:], v[half:, full:]
        if part < 2 * half:
            high = jnp.concatenate(
                [high, jnp.zeros((2 * half - part, width - full), v.dtype)], axis=0
            )
        blocks.append(jnp.concatenate([low, high], axis=1))
    return jnp.concatenate(blocks, axis=0)


def unpack(k_ref, natural, k):
    _, shares, _, _ = k_ref.shape
    taps, depth, width = natural.shape
    depth = width * taps
    unit = depth // (k_ref.shape[0] * shares)
    part = taps * unit
    full, half = width // 128 * 128, half_rows(part)
    for share in range(shares):
        v = k_ref[k, share].astype(jnp.float32)
        base = (k * shares + share) * unit

        def put(low, high, lane, piece):
            for row in range(low, high, 8):
                at = pl.ds(pl.multiple_of(base + row % unit, 8), 8)
                lanes = slice(lane, lane + piece.shape[1])
                natural[row // unit, at, lanes] = piece[row - low : row - low + 8]

        for i in range(full // 128):
            put(0, part, i * 128, v[i * part : (i + 1) * part])
        if full < width:
            rest = v[full // 128 * part :]
            put(0, half, full, rest[:, : width - full])
            put(half, part, full, rest[: part - half, width - full :])


class Stream:
    def __init__(self, place, chunks, lead, hop, land, col, out, bufs, sems):
        self.place, self.chunks, self.lead, self.hop, self.land = place, chunks, lead, hop, land
        self.col, self.out = col, out
        self.col_in, self.joined, self.fwd, self.fwd_in, self.back, self.back_in = bufs
        self.col_sem, self.fwd_sem, self.back_sem, self.mate_sem = sems[:4]
        self.cross_sem, self.pass_sem = sems[4:]

    def to_col(self, k):
        return remote(self.col.at[k], self.col_in.at[k], self.col_sem, k, dp=self.place.across)

    def to_fwd(self, k, up=4):
        return remote(self.fwd.at[k], self.fwd_in.at[k], self.fwd_sem, k, dp=self.place.at + up)

    def to_back(self, k, down=4):
        return remote(self.back.at[k], self.back_in.at[k], self.back_sem, k, dp=self.place.at - down)

    def to_mate(self, k):
        done = self.out.at[k, self.place.share]
        return remote(done, done, self.mate_sem, k, dp=self.place.mate)

    def to_cross(self, k, i):
        done = self.out.at[k, self.place.share]
        return remote(done, done, self.cross_sem.at[i], k, groups=self.place.others[i])

    def to_pass(self, k, i):
        p = self.place
        slot = 2 * lax.rem(p.group + p.groups - 1 - i, p.groups) + p.core
        done = self.out.at[k, slot]
        return remote(done, done, self.pass_sem.at[i], k, dp=p.mate)

    def join_col(self, k):
        self.to_col(k).wait_recv()
        self.joined[k] = self.col[k] + self.col_in[k]

    def go_fwd(self, k):
        p = self.place

        @pl.when(p.z == 0)
        def _():
            self.fwd[k] = self.joined[k]

        @pl.when(p.z > 0)
        def _():
            self.to_fwd(k, -4).wait_recv()
            self.fwd[k] = self.joined[k] + self.fwd_in[k]

        pl.when(p.z < p.last)(lambda: self.to_fwd(k).start())

    def go_back(self, k):
        p = self.place

        @pl.when(p.z == p.last)
        def _():
            self.back[k] = self.joined[k]

        @pl.when(p.z < p.last)
        def _():
            self.to_back(k, -4).wait_recv()
            self.back[k] = self.joined[k] + self.back_in[k]

        pl.when(p.z > 0)(lambda: self.to_back(k).start())

    def finish(self, k):
        p = self.place

        @pl.when(p.z < p.last)
        def _():
            self.out[k, p.share] = self.fwd[k] + self.back_in[k]

        @pl.when(p.z == p.last)
        def _():
            self.out[k, p.share] = self.fwd[k]

        for i in range(p.groups - 1):
            self.to_cross(k, i).start()
        self.to_mate(k).start()

    def pass_on(self, k):
        for i in range(self.place.groups - 1):
            self.to_cross(k, i).wait_recv()
            self.to_pass(k, i).start()

    def arrive(self, k):
        self.to_mate(k).wait_recv()
        for i in range(self.place.groups - 1):
            self.to_pass(k, i).wait_recv()
        self.land(k)

    @staticmethod
    def steps(chunks, lead, hop, last):
        return chunks + lead + (last + 1) * hop + 1

    def step(self, t):
        p, chunks, hop = self.place, self.chunks, self.hop
        t = t - self.lead
        at_step(t, chunks, self.join_col)
        at_step(t - p.z * hop, chunks, self.go_fwd)
        at_step(t - (p.last - p.z) * hop, chunks, self.go_back)
        at_step(t - p.last * hop, chunks, self.finish)
        at_step(t - p.last * hop - hop, chunks, self.pass_on)
        at_step(t - p.last * hop - hop - 1, chunks, self.arrive)

    def drain(self, k):
        p = self.place
        self.to_col(k).wait_send()
        pl.when(p.z < p.last)(lambda: self.to_fwd(k).wait_send())
        pl.when(p.z > 0)(lambda: self.to_back(k).wait_send())
        self.to_mate(k).wait_send()
        for i in range(p.groups - 1):
            self.to_cross(k, i).wait_send()
            self.to_pass(k, i).wait_send()

    @staticmethod
    def scratch(chunks, part, width, groups):
        piece = pltpu.VMEM((chunks, packed_rows(part, width), 128), jnp.bfloat16)
        out = pltpu.VMEM((chunks, 2 * groups, packed_rows(part, width), 128), jnp.bfloat16)
        sems = pltpu.SemaphoreType.DMA((2, chunks))
        many = pltpu.SemaphoreType.DMA((groups - 1, 2, chunks))
        return [piece, out] + [piece] * 6 + [sems] * 4 + [many] * 2


class Edges:
    def __init__(self, place, first, final, out, sem):
        self.place, self.first, self.final, self.out, self.sem = place, first, final, out, sem

    def down(self, k, to=1):
        return remote(self.final(k), self.out(0, k), self.sem.at[0], k, dp=self.place.at + to)

    def up(self, k, to=1):
        return remote(self.first(k), self.out(1, k), self.sem.at[1], k, dp=self.place.at - to)

    def start(self, k):
        at, dp = self.place.at, self.place.dp
        pl.when(at < dp - 1)(lambda: self.down(k).start())
        pl.when(at > 0)(lambda: self.up(k).start())

    def drain(self, k):
        at, dp = self.place.at, self.place.dp

        @pl.when(at < dp - 1)
        def _():
            self.down(k).wait_send()
            self.up(k, -1).wait_recv()

        @pl.when(at > 0)
        def _():
            self.up(k).wait_send()
            self.down(k, -1).wait_recv()


class Renewal:
    def __init__(self, place, mine, which, state, col, scratch):
        self.place, self.mine, self.which, self.state, self.col = place, mine, which, state, col
        self.bufs = scratch[:3]
        self.pair_out, self.pair_in, self.load_sem, self.pair_sem = scratch[3:]

    def loads(self, k):
        src = pl.ds(2 * self.place.group, 2)
        return [
            pltpu.make_async_copy(
                ref.at[self.which, :, k, src], buf.at[k], self.load_sem.at[i, k]
            )
            for i, (ref, buf) in enumerate(zip(self.state, self.bufs))
        ]

    def start(self, k):
        for copy in self.loads(k):
            copy.start()

    def to_pair(self, k):
        return remote(
            self.pair_out.at[k], self.pair_in.at[k], self.pair_sem, k, dp=self.place.mate
        )

    def renew(self, k):
        for copy in self.loads(k):
            copy.wait()
        w, m, g = self.bufs

        def new(c):
            velocity = momentum_decay * m[k, :, c] + g[k, :, c].astype(jnp.float32)
            updated = w[k, :, c].astype(jnp.float32) - learn_rate * velocity
            updated = updated.reshape(-1, updated.shape[-1])
            return packed(jnp.where(self.mine, updated, 0.0)).astype(jnp.bfloat16)

        self.pair_out[k] = new(1 - self.place.core)
        self.to_pair(k).start()
        self.col[k] = new(self.place.core)

    def join(self, k):
        self.to_pair(k).wait_recv()
        self.col[k] = self.col[k] + self.pair_in[k]

    @staticmethod
    def scratch(chunks, taps, unit, width):
        load = lambda dtype: pltpu.VMEM((chunks, taps, 2, unit, width), dtype)
        piece = pltpu.VMEM((chunks, packed_rows(taps * unit, width), 128), jnp.bfloat16)
        return [load(jnp.bfloat16), load(jnp.float32), load(jnp.bfloat16), piece, piece] + [
            pltpu.SemaphoreType.DMA((3, chunks)),
            pltpu.SemaphoreType.DMA((2, chunks)),
        ]


def silu(v):
    return v / (1.0 + jnp.exp2(v * -log2_e))


def spread_rows(d):
    a, b = near * near, far * far
    even_near, odd_near = d[4] - b * d[2], near * (d[3] - b * d[1])
    even_far, odd_far = d[4] - a * d[2], far * (d[3] - a * d[1])
    return (
        d[4] + (a * b) * d[0] - (a + b) * d[2],
        even_near + odd_near,
        even_near - odd_near,
        even_far + odd_far,
        even_far - odd_far,
        d[5] + (a * b) * d[1] - (a + b) * d[3],
    )


def spread_taps(k):
    a, b = near * near, far * far
    n, f = 1.0 / (2.0 * a * (a - b)), 1.0 / (2.0 * b * (b - a))
    even_near, odd_near = n * k[0] + (n * a) * k[2], (n * near) * k[1]
    even_far, odd_far = f * k[0] + (f * b) * k[2], (f * far) * k[1]
    return (
        (1.0 / (a * b)) * k[0],
        even_near + odd_near,
        even_near - odd_near,
        even_far + odd_far,
        even_far - odd_far,
        k[2],
    )


def gather_rows(m):
    a, b = near * near, far * far
    even_near, odd_near = m[1] + m[2], m[1] - m[2]
    even_far, odd_far = m[3] + m[4], m[3] - m[4]
    return (
        m[0] + even_near + even_far,
        near * odd_near + far * odd_far,
        a * even_near + b * even_far,
        (a * near) * odd_near + (b * far) * odd_far + m[5],
    )


parts, rows_out, rows_in = 6, 4, 6


def transform(natural, wide, block):
    taps, _, width = natural.shape
    cols = pl.ds(pl.multiple_of(block * 128, 128), 128)
    for out in range(0, width, 128):
        end = min(out + 128, width)
        k = [natural[tap, cols, out:end].T for tap in range(taps)]
        for j, part in enumerate(spread_taps(k)):
            wide[j, out:end, cols] = part.astype(jnp.bfloat16)


def block_kernel(groups, dp, owners_ref, *refs):
    fine_state, coarse_state, x_ref, y_ref = refs[:3], refs[3:6], refs[6], refs[7]
    scratch = list(refs[8:])

    def take(count):
        taken = scratch[:count]
        del scratch[:count]
        return taken

    act, rims, natural, wide, patch_0, patch_1, acc_0, acc_1 = take(8)
    x_sem, y_sem, x_edge_sem, hidden_edge_sem = take(4)
    one_scratch, two_scratch = take(7), take(7)
    first_scratch, second_scratch = take(14), take(14)

    place = Place(groups, dp)
    at, last = place.at, place.last
    _, images, height, channels, width = act.shape
    units = 2 * images
    taps = natural.shape[0]
    depth = taps * channels
    blocks = -(-depth // 128)
    per_block = 128 * fine_chunks // depth

    def mine(which):
        flag = jnp.where(owners_ref[which] == at, 1.0, 0.0)
        return jnp.full((1, channels), flag, jnp.float32) > 0.5

    def land_first(k):
        unpack(first.out, natural, k)

        @pl.when((k % per_block == per_block - 1) | (k == fine_chunks - 1))
        def _():
            transform(natural, wide, k // per_block)

    def land_second(k):
        unpack(second.out, natural, k)

    first = Stream(
        place, fine_chunks, fine_hop, fine_hop, land_first,
        first_scratch[0], first_scratch[1], first_scratch[2:8], first_scratch[8:],
    )
    second = Stream(
        place, coarse_chunks, coarse_hop, coarse_hop, land_second,
        second_scratch[0], second_scratch[1], second_scratch[2:8], second_scratch[8:],
    )
    one = Renewal(place, mine(0), 0, fine_state, first.col, one_scratch)
    two = Renewal(place, mine(1), 1, coarse_state, second.col, two_scratch)
    x_edges = Edges(
        place, lambda k: x_ref.at[k, 0], lambda k: x_ref.at[k, height - 1],
        lambda side, k: rims.at[0, side, k], x_edge_sem,
    )
    hidden_edges = Edges(
        place, lambda k: act.at[1, k, 0], lambda k: act.at[1, k, height - 1],
        lambda side, k: rims.at[1, side, k], hidden_edge_sem,
    )

    def x_load(k):
        return pltpu.make_async_copy(x_ref.at[k], act.at[0, k], x_sem.at[k])

    def y_store(k):
        return pltpu.make_async_copy(act.at[0, k], y_ref.at[k], y_sem.at[k])

    column = lax.broadcasted_iota(jnp.int32, (16, width), 1)
    not_first = jnp.where(column == 0, 0.0, 1.0).astype(jnp.bfloat16)
    not_last = jnp.where(column == width - 1, 0.0, 1.0).astype(jnp.bfloat16)

    def build(n, patch, e):
        layer, image = n // images, n % images
        lanes = pl.ds(e, 16)
        a = []
        for row in range(-1, height + 1):
            if row < 0:
                v = jnp.where(at > 0, rims[layer, 0, image, lanes].astype(jnp.float32), 0.0)
            elif row == height:
                v = jnp.where(at < dp - 1, rims[layer, 1, image, lanes].astype(jnp.float32), 0.0)
            else:
                v = act[layer, image, row, lanes].astype(jnp.float32)
            a.append(silu(v))
        for q in range(height // rows_out):
            d = a[q * rows_out : q * rows_out + rows_in]
            for j, v in enumerate(spread_rows(d)):
                v = v.astype(jnp.bfloat16)
                before = pltpu.roll(v, 1, 1) * not_first
                after = pltpu.roll(v, width - 1, 1) * not_last
                for tap, part in enumerate((before, v, after)):
                    patch[j, pl.ds(tap * channels + e, 16), q * width : (q + 1) * width] = part

    def settle(n, acc, e):
        layer, image = n // images, n % images
        lanes = pl.ds(e, 16)
        for r, v in enumerate(gather_rows([acc[j, lanes] for j in range(parts)])):
            for q in range(height // rows_out):
                row = q * rows_out + r
                x = act[layer, image, row, lanes].astype(jnp.float32)
                act[1 - layer, image, row, lanes] = (
                    x + v[:, q * width : (q + 1) * width]
                ).astype(jnp.bfloat16)

    slabs = list(range(0, channels, 16))

    def work(n, patch, patch_next, acc, acc_before):
        after, before = jnp.minimum(n + 1, units - 1), jnp.maximum(n - 1, 0)
        for j in range(parts):
            acc[j] = jnp.dot(
                wide[j, :, :depth], patch[j], preferred_element_type=jnp.float32
            )
            for e in slabs[len(slabs) * j // parts : len(slabs) * (j + 1) // parts]:
                build(after, patch_next, e)
                settle(before, acc_before, e)

    fine_steps = pair_hop + Stream.steps(fine_chunks, fine_hop, fine_hop, last)
    coarse_steps = 1 + Stream.steps(coarse_chunks, coarse_hop, coarse_hop, last)
    early = max(coarse_steps - images, 0)
    total = max(fine_steps, early * coarse_stride, edge_start + edge_stride * images)
    coarse_start = total - early * coarse_stride

    each(fine_chunks, one.start)
    each(images, lambda k: x_load(k).start())
    each(coarse_chunks, two.start)
    place.meet()

    def coarse_step(q):
        at_step(q, coarse_chunks, two.renew)

        def join(k):
            two.join(k)
            second.to_col(k).start()

        at_step(q - 1, coarse_chunks, join)
        second.step(q - 1)

    def join_one(k):
        one.join(k)
        first.to_col(k).start()

    def step(t, carry):
        at_step(t, fine_chunks, one.renew)
        at_step(t - pair_hop, fine_chunks, join_one)
        first.step(t - pair_hop)
        at_stride(t - edge_start, edge_stride, images, x_edges.start)
        at_stride(t - coarse_start, coarse_stride, early, coarse_step)

        @pl.when(t == total - build_back)
        def _():
            x_load(0).wait()
            x_edges.drain(0)
            for e in slabs:
                build(0, patch_0, e)

        return carry

    lax.fori_loop(0, total, step, 0)

    def between(n):
        pl.when(n < images)(lambda: coarse_step(early + n))

        @pl.when(n == images)
        def _():
            each(blocks, lambda b: transform(natural, wide, b))

        @pl.when(n + 1 < images)
        def _():
            x_load(n + 1).wait()
            x_edges.drain(n + 1)

        at_step(n + 1 - images, images, hidden_edges.drain)
        at_step(n - 2, images, hidden_edges.start)
        at_step(n - 2 - images, images, lambda k: y_store(k).start())

    def both(t, carry):
        between(2 * t)
        work(2 * t, patch_0, patch_1, acc_0, acc_1)
        between(2 * t + 1)
        work(2 * t + 1, patch_1, patch_0, acc_1, acc_0)
        return carry

    lax.fori_loop(0, images, both, 0)
    y_store(images - 2).start()
    for e in slabs:
        settle(units - 1, acc_1, e)
    y_store(images - 1).start()

    def drain_first(k):
        one.to_pair(k).wait_send()
        first.drain(k)

    def drain_second(k):
        two.to_pair(k).wait_send()
        second.drain(k)

    each(fine_chunks, drain_first)
    each(coarse_chunks, drain_second)
    each(images, lambda k: y_store(k).wait())


def local(images, kernel_weights, kernel_momentum, kernel_grads, owners):
    groups, dp = lax.axis_size("groups"), lax.axis_size("dp")
    x = images.transpose(0, 1, 3, 2)
    _, _, taps, columns, fan_in, fan_out = kernel_weights.shape
    count, height, channels, width = x.shape
    shares, depth = 2 * groups, columns * fan_in
    padded = -(-depth // 128) * 128
    state = (kernel_weights, kernel_momentum, kernel_grads)

    def cut(chunks):
        return [a.reshape(2, taps, chunks, shares, -1, fan_out) for a in state]

    fine, coarse = depth // fine_chunks // shares, depth // coarse_chunks // shares
    any_space = pl.BlockSpec(memory_space=pl.ANY)
    smem = pl.BlockSpec(memory_space=pltpu.SMEM)
    patch = pltpu.VMEM((parts, depth, height // rows_out * width), jnp.bfloat16)
    acc = pltpu.VMEM((parts, channels, height // rows_out * width), jnp.float32)
    y = pl.pallas_call(
        functools.partial(block_kernel, groups, dp),
        out_shape=jax.ShapeDtypeStruct(x.shape, x.dtype),
        in_specs=[smem] + [any_space] * 7,
        out_specs=any_space,
        scratch_shapes=[
            pltpu.VMEM((2,) + x.shape, x.dtype),
            pltpu.VMEM((2, 2, count, channels, width), x.dtype),
            pltpu.VMEM((taps, padded, fan_out), jnp.float32),
            pltpu.VMEM((parts, fan_out, padded), jnp.bfloat16),
            patch, patch, acc, acc,
            pltpu.SemaphoreType.DMA((count,)),
            pltpu.SemaphoreType.DMA((count,)),
            pltpu.SemaphoreType.DMA((2, 2, count)),
            pltpu.SemaphoreType.DMA((2, 2, count)),
        ]
        + Renewal.scratch(fine_chunks, taps, fine, fan_out)
        + Renewal.scratch(coarse_chunks, taps, coarse, fan_out)
        + Stream.scratch(fine_chunks, taps * fine, fan_out, groups)
        + Stream.scratch(coarse_chunks, taps * coarse, fan_out, groups),
        compiler_params=pltpu.CompilerParams(
            collective_id=0, has_side_effects=True, vmem_limit_bytes=60 << 20
        ),
    )(owners, *cut(fine_chunks), *cut(coarse_chunks), x)
    return y.transpose(0, 1, 3, 2)


def solution(mesh):
    placed = (
        P("groups", "dp", None, None),
        P("dp", None, None, None, None, None),
        P("dp", None, None, None, None, None),
        P("dp", None, None, None, None, None),
        P(),
    )
    return jax.shard_map(
        local, mesh=mesh, in_specs=placed, out_specs=P("groups", "dp", None, None), check_vma=False
    )
```

time: 115 us -> 90.9 us (0.79); the launches traced: 115 us -> 89.5 us
  Pallas kernels: 113 us -> 84.3 us
  local copies, waits for them, and re-layouts: 0.65 us -> 5.18 us
    pallas_call x3 -> x1, Pallas kernels: 113 us -> 84.3 us  [local(): pl.pallas_call(functools.partial(block_kernel, groups, dp), out_shape=jax...]
    unnamed x0 -> x1, local copies, waits for them, and re-layouts: none -> 5.18 us
where the time goes in v2:
time: 90.9 us; the launch traced here: 89.5 us
  Pallas kernels  84.3 us (93%)
  local copies, waits for them, and re-layouts  5.18 us (6%)
    pallas_call x1, Pallas kernels, local(): pl.pallas_call(functools.partial(block_kernel, groups, dp), out_shape=jax...  84.3 us
    unnamed x1, local copies, waits for them, and re-layouts  5.18 us

profile of v2, /device:TPU:1, one launch (start us, length us, event | category | flops | bytes accessed | tf_op | source)
XLA Modules:
  0.0 89.5 jit_solution(2265435632206121800)
XLA Ops:
  0.0 84.3 %shard_map.55 = bf16[8,8,320,128]{3,2,1,0:T(8,128)(2,1)} custom-call(s32[2]{0:T(128)} %owners_ref.1, bf16[2,3,15,4,16,320]{5,4,3,2,1,0:T(8,128)(2,1)} %bitcast.11, f32[2,3,15,4,16,320]{5,4,3,2,1,0:T(8,128)} %bitcast.8, bf16[2,3,15,4,16,320]{5,4,3,2,1,0:T(8,128)(2,1)} %bitcast.13, bf16[2,3,5,4,48,320]{5,4,3,2,1,0:T(8,128)(2,1)} %bitcast.12, ...), custom_call_target="tpu_custom_call" | custom-call | tf_op jit(solution)/shard_map/pallas_call | solution.py:601
  84.3 5.2 %copy.7 = bf16[8,8,128,320]{2,3,1,0:T(8,128)(2,1)} copy(bf16[8,8,128,320]{2,3,1,0:T(8,128)(2,1)} %bitcast.10) | data formatting | bytes 10485760
